TPU v7x, 32 devices: a whole 2x2x4 slice. The times are simulated.
32 devices in a mesh: dp: 4 (over y, core), space: 8 (over z, x).
Axes of the slice: x: 2, y: 2, z: 4, core: 2. Of those that a mesh axis runs over, the one named last changes fastest.
Arguments:
- volume: bfloat16 [4, 4, 32, 8, 256], P('dp', None, 'space'), may hold values from -6 to 6
- first_weight: bfloat16 [27, 4, 32], replicated, may hold values from -0.875 to 0.875
- second_weight: bfloat16 [27, 32, 64], replicated, may hold values from -0.4375 to 0.4375
- third_weight: bfloat16 [27, 64, 128], replicated, may hold values from -0.3125 to 0.3125
- feature_cotangent: bfloat16 [4, 128, 4, 32], P('dp', 'space'), may hold values from -0.25 to 0.25
Outputs:
- features: bfloat16 [4, 128, 4, 32], P('dp', 'space')
- first_grad: float32 [27, 4, 32], replicated
- second_grad: float32 [27, 32, 64], replicated
- third_grad: float32 [27, 64, 128], P(None, None, 'space')
All inputs are finite; a program needn't handle non-finite values.
Results may differ from a plain program's by a relative error of at most 0.0057.
Values may be sent and summed in bfloat16 or wider, within the bound.
A program may use at most 64 MiB of HBM per device.

v0:
```python
import functools

import jax
import jax.numpy as jnp
from jax import lax
from jax.experimental import pallas as pl
from jax.experimental.pallas import tpu as pltpu
from jax.sharding import PartitionSpec as P

MESH = pl.DeviceIdType.MESH
F32 = jnp.float32
BF16 = jnp.bfloat16
VM = pl.BlockSpec(memory_space=pltpu.VMEM)
nt = (((1,), (1,)), ((), ()))


def mm(a, b):
    return jnp.dot(a, b, preferred_element_type=F32)


def halves(v):
    hi = v.astype(BF16)
    return hi, (v - hi.astype(F32)).astype(BF16)


def mm2(v, b):
    hi, lo = halves(v)
    return mm(hi, b) + mm(lo, b)


def activate(v):
    e = jnp.exp(-jnp.abs(v))
    d = 1.0 + e
    leaky = 0.3 * v + 0.7 * (jnp.maximum(v, 0.0) + jnp.log1p(e))
    slope = 0.3 + 0.7 * (jnp.where(v >= 0.0, 1.0, e) / d)
    return leaky, slope


def shifts(x, width):
    length = x.shape[1]
    lane = lax.broadcasted_iota(jnp.int32, x.shape, 1)
    column = lane % width
    zero = jnp.zeros_like(x)
    sides = (
        jnp.where(column >= 1, pltpu.roll(x, 1, 1), zero),
        x,
        jnp.where(column < width - 1, pltpu.roll(x, length - 1, 1), zero),
    )
    taps = []
    for dy in range(3):
        for side in sides:
            if dy == 0:
                tap = jnp.where(lane >= width, pltpu.roll(side, width, 1), zero)
            elif dy == 1:
                tap = side
            else:
                tap = jnp.where(
                    lane < length - width, pltpu.roll(side, length - width, 1), zero
                )
            taps.append(tap)
    return taps


def pool_matrix(shape, width, flip=False):
    a = lax.broadcasted_iota(jnp.int32, shape, 1 if flip else 0)
    b = lax.broadcasted_iota(jnp.int32, shape, 0 if flip else 1)
    row = a // (2 * width)
    return (row * (width // 2) + (a % width) // 2 == b).astype(F32).astype(BF16)


def first_kernel(x_ref, w_ref, pooled_ref, slope_ref, taps_ref):
    taps = shifts(x_ref[...].astype(F32), 256)
    taps = jnp.concatenate(taps + [jnp.zeros((40, taps[0].shape[1]), F32)], axis=0)
    taps_ref[...] = taps.astype(BF16)
    active, slope = activate(mm(w_ref[...], taps_ref[...]))
    slope_ref[...] = slope
    deep = jnp.concatenate(
        [active[0:32] + active[32:64], active[64:96] + active[96:128]], axis=0
    )
    pool = pool_matrix((256, 128), 256)
    for y in range(4):
        low = deep[:, y * 512 : y * 512 + 256]
        high = deep[:, y * 512 + 256 : y * 512 + 512]
        pooled_ref[:, y * 128 : y * 128 + 128] = (mm2(low + high, pool) * 0.125).astype(BF16)


def second_kernel(x_ref, w_ref, pooled_ref, slope_ref, taps_ref):
    taps = jnp.concatenate(shifts(x_ref[...].astype(F32), 128), axis=0)
    taps_ref[...] = taps.astype(BF16)
    active, slope = activate(mm(w_ref[...], taps_ref[...]))
    slope_ref[...] = slope
    deep = active[0:64] + active[64:128]
    pool = pool_matrix((512, 128), 128)
    pooled_ref[...] = (mm2(deep, pool) * 0.125).astype(BF16)


def third_kernel(x_ref, w_ref, c_ref, grad_ref, paired_ref, weight_ref):
    taps = jnp.concatenate(shifts(x_ref[...].astype(F32), 64), axis=0).astype(BF16)
    active, slope = activate(mm(w_ref[...], taps))
    paired_ref[...] = mm2(active, pool_matrix((128, 32), 64))
    wide = mm(c_ref[...], pool_matrix((32, 128), 64, True))
    grad = (wide * 0.125 * slope).astype(BF16)
    grad_ref[...] = grad
    taps = jnp.concatenate([taps, jnp.zeros((320, 128), BF16)], axis=0)
    for part in range(4):
        piece = taps[part * 512 : part * 512 + 512]
        weight_ref[part] = lax.dot_general(
            grad, piece, nt, preferred_element_type=F32
        ).astype(BF16)


def fourth_kernel(g_ref, w_ref, slope_ref, taps_ref, grad_ref, weight_ref):
    taps = jnp.concatenate(shifts(g_ref[...].astype(F32), 64), axis=0).astype(BF16)
    back = mm(w_ref[...], taps)
    wide = mm2(back, pool_matrix((128, 512), 128, True)) * 0.125
    grad = (jnp.concatenate([wide, wide], axis=0) * slope_ref[...]).astype(BF16)
    grad_ref[...] = grad
    total = lax.dot_general(grad, taps_ref[...], nt, preferred_element_type=F32)
    total = total[0:64] + pltpu.roll(total[64:128], total.shape[1] - 32, 1)
    for k in range(9):
        weight_ref[k * 64 : k * 64 + 64, :] = total[:, k * 128 : k * 128 + 128]


def fifth_kernel(g_ref, w_ref, slope_ref, taps_ref, weight_ref, grad_ref, wide_ref):
    wide_ref[...] = jnp.concatenate(shifts(g_ref[...].astype(F32), 128), axis=0).astype(BF16)
    back = mm(w_ref[...], wide_ref[...])
    pool = pool_matrix((128, 256), 256, True)
    for y in range(4):
        wide = mm2(back[:, y * 128 : y * 128 + 128], pool) * 0.125
        wide = jnp.concatenate([wide[0:32], wide[0:32], wide[32:64], wide[32:64]], axis=0)
        for part in range(2):
            at = y * 512 + part * 256
            grad_ref[:, at : at + 256] = (wide * slope_ref[:, at : at + 256]).astype(BF16)
    total = lax.dot_general(grad_ref[...], taps_ref[...], nt, preferred_element_type=F32)
    result = total[0:32]
    for z in range(1, 4):
        result = result + pltpu.roll(total[32 * z : 32 * z + 32], 256 - 4 * z, 1)
    weight_ref[...] = jnp.concatenate([result[:, 0:128], result[:, 128:256]], axis=0)


def call(kernel, outs, scratch=()):
    return pl.pallas_call(
        kernel,
        out_shape=[jax.ShapeDtypeStruct(s, d) for s, d in outs],
        out_specs=[VM] * len(outs),
        scratch_shapes=list(scratch),
        compiler_params=pltpu.CompilerParams(vmem_limit_bytes=48 << 20),
    )


def greet(axes):
    barrier = pltpu.get_barrier_semaphore()
    count = 0
    for axis, n in axes:
        me = lax.axis_index(axis)
        for k in range(1, n):
            pl.semaphore_signal(
                barrier, inc=1, device_id={axis: lax.rem(me + k, n)}, device_id_type=MESH
            )
            count += 1
    pl.semaphore_wait(barrier, count)


def spread_to(axis, n, send, recv, source, target):
    me = lax.axis_index(axis)
    copies = []
    for k in range(1, n):
        peer = lax.rem(me + k, n)
        copy = pltpu.make_async_remote_copy(
            src_ref=source(peer),
            dst_ref=target(k),
            send_sem=send.at[k],
            recv_sem=recv.at[k],
            device_id={axis: peer},
            device_id_type=MESH,
        )
        copy.start()
        copies.append(copy)
    return copies


def finish(copies):
    for copy in copies:
        copy.wait()


def reduce_kernel(
    nd, n, a_ref, b_ref, p_ref, a_out, b_out, p_out,
    a_slot, b_slot, a_sum, b_sum, a_next, b_next, b_mid, sends, recvs,
):
    d = lax.axis_index("dp")
    s = lax.axis_index("space")
    greet((("dp", nd), ("space", n)))
    one = spread_to("dp", nd, sends.at[0], recvs.at[0], lambda p: a_ref.at[p], lambda k: a_slot.at[k])
    two = spread_to("dp", nd, sends.at[1], recvs.at[1], lambda p: b_ref.at[p], lambda k: b_slot.at[k])
    six = spread_to("space", n, sends.at[2], recvs.at[2], lambda p: p_ref.at[p], lambda k: p_out.at[s])
    p_out[s] = p_ref[s]
    finish(two)
    total = b_ref[d]
    for k in range(1, nd):
        total = total + b_slot[k]
    b_sum[...] = total
    three = spread_to("space", n, sends.at[3], recvs.at[3], lambda p: b_sum.at[p], lambda k: b_next.at[k])
    finish(one)
    total = a_ref[d].astype(F32)
    for k in range(1, nd):
        total = total + a_slot[k].astype(F32)
    a_sum[...] = total
    four = spread_to("space", n, sends.at[4], recvs.at[4], lambda p: a_sum.at[p], lambda k: a_next.at[k])
    finish(three)
    total = b_sum[s]
    for k in range(1, n):
        total = total + b_next[k]
    b_mid[d] = total
    three = spread_to("dp", nd, sends.at[5], recvs.at[5], lambda p: b_mid.at[d], lambda k: b_mid.at[d])
    finish(three)
    b_out[s] = b_mid[...]
    three = spread_to("space", n, sends.at[6], recvs.at[6], lambda p: b_mid, lambda k: b_out.at[s])
    finish(four)
    total = a_sum[s]
    for k in range(1, n):
        total = total + a_next[k]
    a_out[d] = total
    four = spread_to("dp", nd, sends.at[7], recvs.at[7], lambda p: a_out.at[d], lambda k: a_out.at[d])
    finish(four)
    finish(three)
    finish(six)


def reduce_all(nd, n, a, b, p):
    share = a.shape[2]
    rows = b.shape[2]
    most = max(nd, n)
    return pl.pallas_call(
        functools.partial(reduce_kernel, nd, n),
        out_shape=[
            jax.ShapeDtypeStruct((nd, share, 512), F32),
            jax.ShapeDtypeStruct((n, nd, rows, 128), F32),
            jax.ShapeDtypeStruct(p.shape, F32),
        ],
        in_specs=[VM] * 3,
        out_specs=[VM] * 3,
        scratch_shapes=[
            pltpu.VMEM((nd, n, share, 512), BF16),
            pltpu.VMEM((nd, n, rows, 128), F32),
            pltpu.VMEM((n, share, 512), F32),
            pltpu.VMEM((n, rows, 128), F32),
            pltpu.VMEM((n, share, 512), F32),
            pltpu.VMEM((n, rows, 128), F32),
            pltpu.VMEM((nd, rows, 128), F32),
            pltpu.SemaphoreType.DMA((8, most)),
            pltpu.SemaphoreType.DMA((8, most)),
        ],
        compiler_params=pltpu.CompilerParams(
            collective_id=1, has_side_effects=True, vmem_limit_bytes=48 << 20
        ),
    )(a, b, p)


def banded(weight, planes):
    taps, in_width, out_width = weight.shape
    kernel = weight.reshape(3, 9, in_width, out_width).transpose(3, 1, 0, 2)
    rows = [
        jnp.pad(kernel, ((0, 0), (0, 0), (z, planes - 1 - z), (0, 0))) for z in range(planes)
    ]
    return jnp.stack(rows).reshape(planes * out_width, 9 * (planes + 2) * in_width)


def mirrored(weight):
    return weight[::-1].transpose(0, 2, 1)


def rim(block, n, width):
    forward = [(i, i + 1) for i in range(n - 1)]
    backward = [(target, source) for source, target in forward]
    low = lax.ppermute(block[-width:], "space", forward)
    high = lax.ppermute(block[:width], "space", backward)
    return jnp.concatenate([low, block, high], axis=0)


def body(nd, n, volume, first_weight, second_weight, third_weight, feature_cotangent):
    share = feature_cotangent.shape[1]
    depth = feature_cotangent.shape[2]
    planes = volume[0].transpose(1, 0, 2, 3).reshape(16, 2048)
    weight_one = jnp.pad(banded(first_weight, 4), ((0, 0), (0, 40)))
    weight_two = banded(second_weight, 2)
    weight_three = banded(third_weight, 1)
    flip_three = banded(mirrored(third_weight), 1)
    flip_two = banded(mirrored(second_weight), 2)
    spread = jnp.repeat(feature_cotangent[0], 2, axis=1)
    cotangent = lax.all_to_all(spread, "space", split_axis=1, concat_axis=0, tiled=True)
    cotangent = cotangent.reshape(128, 32)

    pooled_one, slope_one, taps_one = call(
        first_kernel, [((64, 512), BF16), ((128, 2048), F32), ((256, 2048), BF16)]
    )(rim(planes, n, 4), weight_one)
    pooled_two, slope_two, taps_two = call(
        second_kernel, [((64, 128), BF16), ((128, 512), F32), ((1152, 512), BF16)]
    )(rim(pooled_one, n, 32), weight_two)
    grad_three, paired, part_three = call(
        third_kernel, [((128, 128), BF16), ((128, 32), F32), ((4, 128, 512), BF16)]
    )(rim(pooled_two, n, 64), weight_three, cotangent)
    grad_two, part_two = call(
        fourth_kernel, [((128, 512), BF16), ((576, 128), F32)]
    )(rim(grad_three, n, 128), flip_three, slope_two, taps_two)
    (part_one,) = call(
        fifth_kernel,
        [((64, 128), F32)],
        [pltpu.VMEM((128, 2048), BF16), pltpu.VMEM((2304, 512), BF16)],
    )(rim(grad_two, n, 64), flip_two, slope_one, taps_one)

    parts = jnp.concatenate([part_two, part_one, jnp.zeros((384, 128), F32)], axis=0)
    third, rest, turned = reduce_all(
        nd,
        n,
        part_three.reshape(nd, n, share, 2048 // nd),
        parts.reshape(nd, n, 1024 // (nd * n), 128),
        paired.reshape(n, share, 32),
    )
    features = turned.reshape(depth, 2, share, 32).sum(axis=1) * 0.125
    features = features.transpose(1, 0, 2).astype(BF16)[None]
    third = third.transpose(1, 0, 2).reshape(share, 2048)[:, :1728]
    third_grad = third.reshape(share, 9, 3, 64).transpose(2, 1, 3, 0).reshape(27, 64, share)
    rest = rest.transpose(1, 0, 2, 3).reshape(1024, 128)
    second = rest[:576].reshape(9, 64, 4, 32)[:, :, :3]
    second_grad = second.transpose(2, 0, 3, 1).reshape(27, 32, 64)
    first = rest[576:640].reshape(2, 32, 128).transpose(1, 0, 2).reshape(32, 256)
    first = first[:, :216].reshape(32, 9, 6, 4)[:, :, :3]
    first_grad = first.transpose(2, 1, 3, 0).reshape(27, 4, 32)
    return (features, first_grad, second_grad, third_grad)


def solution(mesh):
    return jax.shard_map(
        functools.partial(body, mesh.shape["dp"], mesh.shape["space"]),
        mesh=mesh,
        in_specs=(P("dp", None, "space", None, None), P(), P(), P(), P("dp", "space", None, None)),
        out_specs=(P("dp", "space", None, None), P(), P(), P(None, None, "space")),
        check_vma=False,
    )
```

profile of v0, /device:TPU:26, one launch (start us, length us, event | category | flops | bytes accessed | tf_op | source)
XLA Modules:
  0.0 111.0 jit_solution(2265468622263365742)
XLA Ops:
  0.6 0.8 slice_bitcast_fusion.3
  1.4 1.3 %collective-permute-start = (bf16[4,2048]{1,0:T(4,128)(2,1)S(1)}, bf16[4,2048]{1,0:T(4,128)(2,1)S(1)}, u32[]{:S(2)}, u32[]{:S(2)}) collective-permute-start(bf16[4,2048]{1,0:T(4,128)(2,1)S(1)} %bitcast.130), channel_id=1, source_target_pairs={{0,1},{1,2},{2,3},{3,4},{4,5},{5,6},{6,7},{8,9},{9,10},{10,11},{11... | collective-permute-start | bytes 49160 | tf_op jit(solution)/shard_map/ppermute | solution.py:276
  2.8 4.5 %collective-permute-start.1 = (bf16[4,2048]{1,0:T(4,128)(2,1)S(1)}, bf16[4,2048]{1,0:T(4,128)(2,1)S(1)}, u32[]{:S(2)}, u32[]{:S(2)}) collective-permute-start(bf16[4,2048]{1,0:T(4,128)(2,1)S(1)} %bitcast.131), channel_id=1, source_target_pairs={{1,0},{2,1},{3,2},{4,3},{5,4},{6,5},{7,6},{9,8},{10,9},{11,10},{12... | collective-permute-start | bytes 49160 | tf_op jit(solution)/shard_map/ppermute | solution.py:277
  7.3 1.0 pad_bitcast_fusion.7
  8.3 1.1 %pad_bitcast_fusion.3 = (bf16[1,64,9,4,32]{1,4,2,3,0:T(8,128)(2,1)S(1)}, bf16[1,64,9,4,32]{1,4,2,3,0:T(8,128)(2,1)S(1)}) fusion(bf16[64,9,3,32]{0,3,1,2:T(8,128)(2,1)} %bitcast.113), kind=kLoop, calls=%fused_computation.9 | loop fusion | bytes 405504 | tf_op jit(solution)/shard_map/stack | solution.py:266
  10.2 1.3 %shard_map.84 = (bf16[64,512]{1,0:T(8,128)(2,1)S(1)}, f32[128,2048]{1,0:T(8,128)S(1)}, bf16[256,2048]{1,0:T(8,128)(2,1)S(1)}) custom-call(bf16[24,2048]{1,0:T(8,128)(2,1)S(1)} %pad_maximum_fusion.5.x_ref, bf16[128,256]{1,0:T(8,128)(2,1)S(1)} %pad.40.w_ref), custom_call_target="tpu_custom_call" | custom-call | tf_op jit(solution)/shard_map/pallas_call | solution.py:294
  11.5 1.0 copy-done
  12.5 1.3 %collective-permute-start.2 = (bf16[32,512]{1,0:T(8,128)(2,1)S(1)}, bf16[32,512]{1,0:T(8,128)(2,1)S(1)}, u32[]{:S(2)}, u32[]{:S(2)}) collective-permute-start(bf16[32,512]{1,0:T(8,128)(2,1)S(1)} %get-tuple-element.42), channel_id=1, source_target_pairs={{0,1},{1,2},{2,3},{3,4},{4,5},{5,6},{6,7},{8,9},{9,10},{10,11},{11... | collective-permute-start | bytes 98312 | tf_op jit(solution)/shard_map/ppermute | solution.py:276
  13.8 4.5 %collective-permute-start.3 = (bf16[32,512]{1,0:T(8,128)(2,1)S(1)}, bf16[32,512]{1,0:T(8,128)(2,1)S(1)}, u32[]{:S(2)}, u32[]{:S(2)}) collective-permute-start(bf16[32,512]{1,0:T(8,128)(2,1)S(1)} %get-tuple-element.43), channel_id=1, source_target_pairs={{1,0},{2,1},{3,2},{4,3},{5,4},{6,5},{7,6},{9,8},{10,9},{11,10},{12... | collective-permute-start | bytes 98312 | tf_op jit(solution)/shard_map/ppermute | solution.py:277
  19.9 0.9 shard_map.85
  21.5 1.3 %collective-permute-start.4 = (bf16[64,128]{1,0:T(8,128)(2,1)S(1)}, bf16[64,128]{1,0:T(8,128)(2,1)S(1)}, u32[]{:S(2)}, u32[]{:S(2)}) collective-permute-start(bf16[64,128]{1,0:T(8,128)(2,1)S(1)} %get-tuple-element.19), channel_id=1, source_target_pairs={{0,1},{1,2},{2,3},{3,4},{4,5},{5,6},{6,7},{8,9},{9,10},{10,11},{11... | collective-permute-start | bytes 49160 | tf_op jit(solution)/shard_map/ppermute | solution.py:276
  22.8 4.9 %collective-permute-start.5 = (bf16[64,128]{1,0:T(8,128)(2,1)S(1)}, bf16[64,128]{1,0:T(8,128)(2,1)S(1)}, u32[]{:S(2)}, u32[]{:S(2)}) collective-permute-start(bf16[64,128]{1,0:T(8,128)(2,1)S(1)} %get-tuple-element.19), channel_id=1, source_target_pairs={{1,0},{2,1},{3,2},{4,3},{5,4},{6,5},{7,6},{9,8},{10,9},{11,10},{12... | collective-permute-start | bytes 49160 | tf_op jit(solution)/shard_map/ppermute | solution.py:277
  28.4 8.3 %all-to-all-start = ((bf16[8,2,256]{2,1,0:T(2,128)(2,1)}), bf16[8,2,256]{2,1,0:T(2,128)(2,1)S(1)}, u32[]{:S(2)}, u32[]{:S(2)}) async-start(bf16[8,2,256]{2,1,0:T(2,128)(2,1)} %reshape.111), calls=%async_computation | async-start | bytes 16384 | tf_op jit(solution)/shard_map/all_to_all | solution.py:291
  36.7 0.8 copy.83
  37.5 1.2 %copy.85.w_ref = bf16[128,1728]{1,0:T(8,128)(2,1)S(1)} copy(bf16[128,1728]{0,1:T(8,128)(2,1)} %bitcast.107) | data formatting | bytes 884736 | tf_op jit(solution)/shard_map/reshape;stack | solution.py:266
  38.8 0.9 copy.108
  39.8 0.8 shard_map.86
  40.6 1.3 %collective-permute-start.6 = (bf16[128,128]{1,0:T(8,128)(2,1)S(1)}, bf16[128,128]{1,0:T(8,128)(2,1)S(1)}, u32[]{:S(2)}, u32[]{:S(2)}) collective-permute-start(bf16[128,128]{1,0:T(8,128)(2,1)S(1)} %get-tuple-element.21), channel_id=1, source_target_pairs={{0,1},{1,2},{2,3},{3,4},{4,5},{5,6},{6,7},{8,9},{9,10},{10,11},{11... | collective-permute-start | bytes 98312 | tf_op jit(solution)/shard_map/ppermute | solution.py:276
  41.9 4.5 %collective-permute-start.7 = (bf16[128,128]{1,0:T(8,128)(2,1)S(1)}, bf16[128,128]{1,0:T(8,128)(2,1)S(1)}, u32[]{:S(2)}, u32[]{:S(2)}) collective-permute-start(bf16[128,128]{1,0:T(8,128)(2,1)S(1)} %get-tuple-element.21), channel_id=1, source_target_pairs={{1,0},{2,1},{3,2},{4,3},{5,4},{6,5},{7,6},{9,8},{10,9},{11,10},{12... | collective-permute-start | bytes 98312 | tf_op jit(solution)/shard_map/ppermute | solution.py:277
  46.4 2.3 %pad_bitcast_fusion.1 = (bf16[1,32,9,4,64]{4,3,2,1,0:T(4,128)(2,1)}, bf16[1,32,9,4,64]{4,3,2,1,0:T(4,128)(2,1)}) fusion(bf16[32,9,3,64]{3,2,1,0:T(4,128)(2,1)} %bitcast.111), kind=kLoop, calls=%fused_computation.7 | loop fusion | bytes 405504 | tf_op jit(solution)/shard_map/stack | solution.py:266
  48.7 1.0 rev.6
  49.8 1.2 %copy.107 = bf16[3,9,128,64]{2,0,1,3:T(4,128)(2,1)} copy(bf16[3,9,128,64]{2,3,1,0:T(8,128)(2,1)S(1)} %bitcast.108) | data formatting | bytes 884736 | tf_op jit(solution)/shard_map/reshape | solution.py:262
  51.0 1.5 %reshape_stack.7.w_ref = bf16[64,3456]{1,0:T(8,128)(2,1)S(1)} reshape(bf16[64,9,3,128]{3,2,1,0:T(4,128)(2,1)} %bitcast.105) | data formatting | bytes 884736 | tf_op jit(solution)/shard_map/reshape;stack | solution.py:266
  52.5 0.9 copy-done.5
  53.4 1.1 %shard_map.87 = (bf16[128,512]{1,0:T(8,128)(2,1)S(1)}, f32[576,128]{1,0:T(8,128)S(1)}) custom-call(bf16[384,128]{1,0:T(8,128)(2,1)S(1)} %pad_maximum_fusion.6.g_ref, bf16[64,3456]{1,0:T(8,128)(2,1)S(1)} %reshape_stack.7.w_ref, f32[128,512]{1,0:T(8,128)S(1)} %copy-done.5, bf16[1152,512]{1,0:T(8,128)(2,1)S(1)} %get-tuple-element.23.taps_ref), custom_call_target="tpu_custom_call" | custom-call | tf_op jit(solution)/shard_map/pallas_call | solution.py:303
  55.3 1.3 %collective-permute-start.8 = (bf16[64,512]{1,0:T(8,128)(2,1)S(1)}, bf16[64,512]{1,0:T(8,128)(2,1)S(1)}, u32[]{:S(2)}, u32[]{:S(2)}) collective-permute-start(bf16[64,512]{1,0:T(8,128)(2,1)S(1)} %get-tuple-element.40), channel_id=1, source_target_pairs={{0,1},{1,2},{2,3},{3,4},{4,5},{5,6},{6,7},{8,9},{9,10},{10,11},{11... | collective-permute-start | bytes 196616 | tf_op jit(solution)/shard_map/ppermute | solution.py:276
  56.6 4.5 %collective-permute-start.9 = (bf16[64,512]{1,0:T(8,128)(2,1)S(1)}, bf16[64,512]{1,0:T(8,128)(2,1)S(1)}, u32[]{:S(2)}, u32[]{:S(2)}) collective-permute-start(bf16[64,512]{1,0:T(8,128)(2,1)S(1)} %get-tuple-element.41), channel_id=1, source_target_pairs={{1,0},{2,1},{3,2},{4,3},{5,4},{6,5},{7,6},{9,8},{10,9},{11,10},{12... | collective-permute-start | bytes 196616 | tf_op jit(solution)/shard_map/ppermute | solution.py:277
  61.2 1.3 %pad_maximum_fusion.1 = bf16[2,32,9,4,64]{4,3,2,1,0:T(4,128)(2,1)} fusion(bf16[1,32,9,4,64]{4,3,2,1,0:T(4,128)(2,1)S(1)} %copy-done.8, bf16[1,32,9,4,64]{4,3,2,1,0:T(4,128)(2,1)S(1)} %copy-done.7), kind=kLoop, calls=%fused_computation.2 | loop fusion | flops 147456 | bytes 589824 | tf_op jit(solution)/shard_map/stack | solution.py:266
  62.5 1.5 %reshape.97.w_ref = bf16[64,2304]{1,0:T(8,128)(2,1)S(1)} reshape(bf16[2,32,9,4,64]{4,3,2,1,0:T(4,128)(2,1)} %pad_maximum_fusion.1) | data formatting | bytes 589824 | tf_op jit(solution)/shard_map/reshape | solution.py:266
  64.1 1.2 %shard_map.88 = f32[64,128]{1,0:T(8,128)S(1)} custom-call(bf16[256,512]{1,0:T(8,128)(2,1)S(1)} %pad_maximum_fusion.2.g_ref, bf16[64,2304]{1,0:T(8,128)(2,1)S(1)} %reshape.97.w_ref, f32[128,2048]{1,0:T(8,128)S(1)} %get-tuple-element.26.slope_ref, bf16[256,2048]{1,0:T(8,128)(2,1)S(1)} %copy-done.1), custom_call_target="tpu_custom_call" | custom-call | tf_op jit(solution)/shard_map/pallas_call | solution.py:306
  65.5 41.8 %shard_map.89 = (f32[4,16,512]{2,1,0:T(8,128)S(1)}, f32[8,4,32,128]{3,2,1,0:T(8,128)S(1)}, f32[8,16,32]{2,1,0:T(8,128)S(1)}) custom-call(bf16[4,8,16,512]{3,2,1,0:T(8,128)(2,1)S(1)} %bitcast.100, f32[4,8,32,128]{3,2,1,0:T(8,128)S(1)} %bitcast.99, f32[8,16,32]{2,1,0:T(8,128)S(1)} %bitcast.104), custom_call_target="tpu_custom_call" | custom-call | tf_op jit(solution)/shard_map/pallas_call | solution.py:234
  107.8 0.9 copy.93
  (79 shorter events, 7.4 us)
Async XLA Ops:
  0.6 9.1 %copy-start.10 = (bf16[1,4,4,8,256]{4,3,2,1,0:T(8,128)(2,1)S(1)}, bf16[1,4,4,8,256]{4,3,2,1,0:T(8,128)(2,1)}, u32[]{:S(2)}) copy-start(bf16[1,4,4,8,256]{4,3,2,1,0:T(8,128)(2,1)} %param.5) | copy-start | bytes 196612
  1.4 8.7 %collective-permute-start = (bf16[4,2048]{1,0:T(4,128)(2,1)S(1)}, bf16[4,2048]{1,0:T(4,128)(2,1)S(1)}, u32[]{:S(2)}, u32[]{:S(2)}) collective-permute-start(bf16[4,2048]{1,0:T(4,128)(2,1)S(1)} %bitcast.130), channel_id=1, source_target_pairs={{0,1},{1,2},{2,3},{3,4},{4,5},{5,6},{6,7},{8,9},{9,10},{10,11},{11... | collective-permute-start | bytes 49160 | tf_op jit(solution)/shard_map/ppermute | solution.py:276
  2.8 7.4 %collective-permute-start.1 = (bf16[4,2048]{1,0:T(4,128)(2,1)S(1)}, bf16[4,2048]{1,0:T(4,128)(2,1)S(1)}, u32[]{:S(2)}, u32[]{:S(2)}) collective-permute-start(bf16[4,2048]{1,0:T(4,128)(2,1)S(1)} %bitcast.131), channel_id=1, source_target_pairs={{1,0},{2,1},{3,2},{4,3},{5,4},{6,5},{7,6},{9,8},{10,9},{11,10},{12... | collective-permute-start | bytes 49160 | tf_op jit(solution)/shard_map/ppermute | solution.py:277
  11.5 1.0 copy-start
  12.5 7.1 %collective-permute-start.2 = (bf16[32,512]{1,0:T(8,128)(2,1)S(1)}, bf16[32,512]{1,0:T(8,128)(2,1)S(1)}, u32[]{:S(2)}, u32[]{:S(2)}) collective-permute-start(bf16[32,512]{1,0:T(8,128)(2,1)S(1)} %get-tuple-element.42), channel_id=1, source_target_pairs={{0,1},{1,2},{2,3},{3,4},{4,5},{5,6},{6,7},{8,9},{9,10},{10,11},{11... | collective-permute-start | bytes 98312 | tf_op jit(solution)/shard_map/ppermute | solution.py:276
  13.8 6.1 %collective-permute-start.3 = (bf16[32,512]{1,0:T(8,128)(2,1)S(1)}, bf16[32,512]{1,0:T(8,128)(2,1)S(1)}, u32[]{:S(2)}, u32[]{:S(2)}) collective-permute-start(bf16[32,512]{1,0:T(8,128)(2,1)S(1)} %get-tuple-element.43), channel_id=1, source_target_pairs={{1,0},{2,1},{3,2},{4,3},{5,4},{6,5},{7,6},{9,8},{10,9},{11,10},{12... | collective-permute-start | bytes 98312 | tf_op jit(solution)/shard_map/ppermute | solution.py:277
  19.1 8.6 %copy-start.11 = (bf16[1,16,4,32]{3,2,1,0:T(4,128)(2,1)S(1)}, bf16[1,16,4,32]{3,2,1,0:T(4,128)(2,1)}, u32[]{:S(2)}) copy-start(bf16[1,16,4,32]{3,2,1,0:T(4,128)(2,1)} %param.9) | copy-start | bytes 12292
  19.1 17.6 %copy-start.9 = (bf16[27,32,64]{2,1,0:T(8,128)(2,1)S(1)}, bf16[27,32,64]{2,1,0:T(8,128)(2,1)}, u32[]{:S(2)}) copy-start(bf16[27,32,64]{2,1,0:T(8,128)(2,1)} %param.7) | copy-start | bytes 331780
  19.1 17.6 %copy-start.6 = (bf16[27,64,128]{2,1,0:T(8,128)(2,1)S(1)}, bf16[27,64,128]{2,1,0:T(8,128)(2,1)}, u32[]{:S(2)}) copy-start(bf16[27,64,128]{2,1,0:T(8,128)(2,1)} %param.8) | copy-start | bytes 1327108
  20.8 0.7 copy-start.4
  21.5 18.2 %collective-permute-start.4 = (bf16[64,128]{1,0:T(8,128)(2,1)S(1)}, bf16[64,128]{1,0:T(8,128)(2,1)S(1)}, u32[]{:S(2)}, u32[]{:S(2)}) collective-permute-start(bf16[64,128]{1,0:T(8,128)(2,1)S(1)} %get-tuple-element.19), channel_id=1, source_target_pairs={{0,1},{1,2},{2,3},{3,4},{4,5},{5,6},{6,7},{8,9},{9,10},{10,11},{11... | collective-permute-start | bytes 49160 | tf_op jit(solution)/shard_map/ppermute | solution.py:276
  22.8 16.9 %collective-permute-start.5 = (bf16[64,128]{1,0:T(8,128)(2,1)S(1)}, bf16[64,128]{1,0:T(8,128)(2,1)S(1)}, u32[]{:S(2)}, u32[]{:S(2)}) collective-permute-start(bf16[64,128]{1,0:T(8,128)(2,1)S(1)} %get-tuple-element.19), channel_id=1, source_target_pairs={{1,0},{2,1},{3,2},{4,3},{5,4},{6,5},{7,6},{9,8},{10,9},{11,10},{12... | collective-permute-start | bytes 49160 | tf_op jit(solution)/shard_map/ppermute | solution.py:277
  28.4 11.2 %all-to-all-start = ((bf16[8,2,256]{2,1,0:T(2,128)(2,1)}), bf16[8,2,256]{2,1,0:T(2,128)(2,1)S(1)}, u32[]{:S(2)}, u32[]{:S(2)}) async-start(bf16[8,2,256]{2,1,0:T(2,128)(2,1)} %reshape.111), calls=%async_computation | async-start | bytes 16384 | tf_op jit(solution)/shard_map/all_to_all | solution.py:291
  40.6 11.9 %collective-permute-start.6 = (bf16[128,128]{1,0:T(8,128)(2,1)S(1)}, bf16[128,128]{1,0:T(8,128)(2,1)S(1)}, u32[]{:S(2)}, u32[]{:S(2)}) collective-permute-start(bf16[128,128]{1,0:T(8,128)(2,1)S(1)} %get-tuple-element.21), channel_id=1, source_target_pairs={{0,1},{1,2},{2,3},{3,4},{4,5},{5,6},{6,7},{8,9},{9,10},{10,11},{11... | collective-permute-start | bytes 98312 | tf_op jit(solution)/shard_map/ppermute | solution.py:276
  41.9 10.6 %collective-permute-start.7 = (bf16[128,128]{1,0:T(8,128)(2,1)S(1)}, bf16[128,128]{1,0:T(8,128)(2,1)S(1)}, u32[]{:S(2)}, u32[]{:S(2)}) collective-permute-start(bf16[128,128]{1,0:T(8,128)(2,1)S(1)} %get-tuple-element.21), channel_id=1, source_target_pairs={{1,0},{2,1},{3,2},{4,3},{5,4},{6,5},{7,6},{9,8},{10,9},{11,10},{12... | collective-permute-start | bytes 98312 | tf_op jit(solution)/shard_map/ppermute | solution.py:277
  52.5 1.0 copy-start.5
  53.4 7.7 %copy-start.7 = (bf16[1,32,9,4,64]{4,3,2,1,0:T(4,128)(2,1)S(1)}, bf16[1,32,9,4,64]{4,3,2,1,0:T(4,128)(2,1)}, u32[]{:S(2)}) copy-start(bf16[1,32,9,4,64]{4,3,2,1,0:T(4,128)(2,1)} %get-tuple-element.36) | copy-start | bytes 442372
  53.4 7.7 %copy-start.8 = (bf16[1,32,9,4,64]{4,3,2,1,0:T(4,128)(2,1)S(1)}, bf16[1,32,9,4,64]{4,3,2,1,0:T(4,128)(2,1)}, u32[]{:S(2)}) copy-start(bf16[1,32,9,4,64]{4,3,2,1,0:T(4,128)(2,1)} %get-tuple-element.37) | copy-start | bytes 442372
  54.6 0.7 copy-start.2
  55.3 8.7 %collective-permute-start.8 = (bf16[64,512]{1,0:T(8,128)(2,1)S(1)}, bf16[64,512]{1,0:T(8,128)(2,1)S(1)}, u32[]{:S(2)}, u32[]{:S(2)}) collective-permute-start(bf16[64,512]{1,0:T(8,128)(2,1)S(1)} %get-tuple-element.40), channel_id=1, source_target_pairs={{0,1},{1,2},{2,3},{3,4},{4,5},{5,6},{6,7},{8,9},{9,10},{10,11},{11... | collective-permute-start | bytes 196616 | tf_op jit(solution)/shard_map/ppermute | solution.py:276
  56.6 7.4 %collective-permute-start.9 = (bf16[64,512]{1,0:T(8,128)(2,1)S(1)}, bf16[64,512]{1,0:T(8,128)(2,1)S(1)}, u32[]{:S(2)}, u32[]{:S(2)}) collective-permute-start(bf16[64,512]{1,0:T(8,128)(2,1)S(1)} %get-tuple-element.41), channel_id=1, source_target_pairs={{1,0},{2,1},{3,2},{4,3},{5,4},{6,5},{7,6},{9,8},{10,9},{11,10},{12... | collective-permute-start | bytes 196616 | tf_op jit(solution)/shard_map/ppermute | solution.py:277
  61.2 2.9 %copy-start.1 = (bf16[256,2048]{1,0:T(8,128)(2,1)S(1)}, bf16[256,2048]{1,0:T(8,128)(2,1)}, u32[]{:S(2)}) copy-start(bf16[256,2048]{1,0:T(8,128)(2,1)} %copy-done) | copy-start | bytes 3145732
  64.1 1.2 %copy-start.3 = (f32[576,128]{1,0:T(8,128)S(1)}, f32[576,128]{1,0:T(8,128)}, u32[]{:S(2)}) copy-start(f32[576,128]{1,0:T(8,128)} %copy-done.2) | copy-start | bytes 884740
where the time goes:
time: 112 us; the launch traced here: 111 us
  Pallas kernels  47.1 us (42%)
  starting transfers between devices  37.8 us (34%)
  local copies, waits for them, and re-layouts  22.6 us (20%)
  other arithmetic  1.95 us (2%)
  between operations  1.23 us (1%)
    pallas_call x1, Pallas kernels, reduce_all(): pl.pallas_call(functools.partial(reduce_kernel, nd, n), out_shape=[jax.Sh...  41.8 us
    ppermute x5, starting transfers between devices, rim(): high = lax.ppermute(block[:width], 'space', backward)  23.1 us
    all_to_all x1, starting transfers between devices, body(): lax.all_to_all(spread, 'space', split_axis=1, concat_axis=0, tiled=True)  8.31 us
    another operation x7, local copies, waits for them, and re-layouts, banded(): jnp.stack(rows).reshape(planes * out_width, 9 * (planes + 2) * in_width)  7.83 us
    ppermute x5, starting transfers between devices, rim(): low = lax.ppermute(block[-width:], 'space', forward)  6.44 us
    unnamed x32, local copies, waits for them, and re-layouts  5.58 us
  transfers between devices with their start and end apart: 11, of which 1 were waited for; matrix products, arithmetic and copies ran while one was open for 15% of the time, Pallas kernels for 0%

commit v1 on v0

v1 whole, which is shorter than its diff:
```python
import functools

import jax
import jax.numpy as jnp
from jax import lax
from jax.experimental import pallas as pl
from jax.experimental.pallas import tpu as pltpu
from jax.sharding import PartitionSpec as P

MESH = pl.DeviceIdType.MESH
F32 = jnp.float32
BF16 = jnp.bfloat16
VM = pl.BlockSpec(memory_space=pltpu.VMEM)
nt = (((1,), (1,)), ((), ()))


def mm(a, b):
    return jnp.dot(a, b, preferred_element_type=F32)


def halves(v):
    hi = v.astype(BF16)
    return hi, (v - hi.astype(F32)).astype(BF16)


def mm2(v, b):
    hi, lo = halves(v)
    return mm(hi, b) + mm(lo, b)


def activate(v):
    e = jnp.exp(-jnp.abs(v))
    d = 1.0 + e
    leaky = 0.3 * v + 0.7 * (jnp.maximum(v, 0.0) + jnp.log1p(e))
    slope = 0.3 + 0.7 * (jnp.where(v >= 0.0, 1.0, e) / d)
    return leaky, slope


def shifts(x, width):
    length = x.shape[1]
    lane = lax.broadcasted_iota(jnp.int32, x.shape, 1)
    column = lane % width
    zero = jnp.zeros_like(x)
    sides = (
        jnp.where(column >= 1, pltpu.roll(x, 1, 1), zero),
        x,
        jnp.where(column < width - 1, pltpu.roll(x, length - 1, 1), zero),
    )
    taps = []
    for dy in range(3):
        for side in sides:
            if dy == 0:
                tap = jnp.where(lane >= width, pltpu.roll(side, width, 1), zero)
            elif dy == 1:
                tap = side
            else:
                tap = jnp.where(
                    lane < length - width, pltpu.roll(side, length - width, 1), zero
                )
            taps.append(tap)
    return taps


def pool_matrix(shape, width, flip=False):
    a = lax.broadcasted_iota(jnp.int32, shape, 1 if flip else 0)
    b = lax.broadcasted_iota(jnp.int32, shape, 0 if flip else 1)
    row = a // (2 * width)
    return (row * (width // 2) + (a % width) // 2 == b).astype(F32).astype(BF16)


def tn(a, b):
    return lax.dot_general(a, b, (((0,), (0,)), ((), ())), preferred_element_type=F32)


def mnt(a, b):
    return lax.dot_general(a, b, nt, preferred_element_type=F32)


def greet(axes):
    barrier = pltpu.get_barrier_semaphore()
    count = 0
    for axis, n in axes:
        me = lax.axis_index(axis)
        for k in range(1, n):
            pl.semaphore_signal(
                barrier, inc=1, device_id={axis: lax.rem(me + k, n)}, device_id_type=MESH
            )
            count += 1
    pl.semaphore_wait(barrier, count)


def spread_to(axis, n, send, recv, source, target):
    me = lax.axis_index(axis)
    copies = []
    for k in range(1, n):
        peer = lax.rem(me + k, n)
        copy = pltpu.make_async_remote_copy(
            src_ref=source(peer),
            dst_ref=target,
            send_sem=send.at[k],
            recv_sem=recv.at[k],
            device_id={axis: peer},
            device_id_type=MESH,
        )
        copy.start()
        copies.append(copy)
    return copies


def finish(copies):
    for copy in copies:
        copy.wait()


def added(slots, count):
    total = slots[0].astype(F32)
    for k in range(1, count):
        total = total + slots[k].astype(F32)
    return total


class Halo:
    def __init__(self, n, send, recv, first, last, low, high):
        s = lax.axis_index("space")
        self.has_low, self.has_high = s > 0, s < n - 1
        self.up = pltpu.make_async_remote_copy(
            src_ref=last, dst_ref=low, send_sem=send.at[0], recv_sem=recv.at[0],
            device_id={"space": lax.rem(s + 1, n)}, device_id_type=MESH,
        )
        self.down = pltpu.make_async_remote_copy(
            src_ref=first, dst_ref=high, send_sem=send.at[1], recv_sem=recv.at[1],
            device_id={"space": lax.rem(s + n - 1, n)}, device_id_type=MESH,
        )

        @pl.when(self.has_high)
        def _():
            self.up.start()

        @pl.when(self.has_low)
        def _():
            self.down.start()

        @pl.when(s == 0)
        def _():
            low[...] = jnp.zeros_like(low)

        @pl.when(s == n - 1)
        def _():
            high[...] = jnp.zeros_like(high)

    def wait(self):
        @pl.when(self.has_high)
        def _():
            self.down.wait_recv()

        @pl.when(self.has_low)
        def _():
            self.up.wait_recv()

        @pl.when(self.has_high)
        def _():
            self.up.wait_send()

        @pl.when(self.has_low)
        def _():
            self.down.wait_send()


def lay_taps(into, at, block, width):
    taps = jnp.concatenate(shifts(block.astype(F32), width), axis=0).astype(BF16)
    into[at : at + taps.shape[0], :] = taps


def step_kernel(
    nd, n, share, volume, weight_one, weight_two, weight_three, cotangent,
    a_out, b_out, c_out, p_out,
    rim_zero, rim_one, rim_two, rim_three, rim_four, cot_all,
    taps_one, taps_two, taps_three, wide_three, wide_two, slope_one, grad_one, back_two,
    p_src, a_src, a_slot, a_sum, a_next, b_src, b_slot, b_sum, b_next, b_mid,
    c_src, c_slot, c_sum, c_next, halo_send, halo_recv, sends, recvs,
):
    d = lax.axis_index("dp")
    s = lax.axis_index("space")
    greet((("dp", nd), ("space", n)))

    def halo(index, first, last, low, high):
        return Halo(n, halo_send.at[index], halo_recv.at[index], first, last, low, high)

    def spread(index, axis, source, target):
        return spread_to(
            axis, nd if axis == "dp" else n, sends.at[index], recvs.at[index], source, target
        )

    edge = halo(0, volume.at[0], volume.at[3], rim_zero.at[0], rim_zero.at[1])
    cot_all[s] = cotangent[lax.div(s, 2)]
    cots = spread(0, "space", lambda p: cotangent.at[lax.div(p, 2)], cot_all.at[s])
    for t in range(27):
        back_two[:, t * 64 : t * 64 + 64] = weight_two[26 - t]
    taps_two[1152:1184, :] = jnp.zeros((32, 512), BF16)
    taps_three[1728:2048, :] = jnp.zeros((320, 128), BF16)
    edge.wait()

    planes = [rim_zero[0]] + [volume[z] for z in range(4)] + [rim_zero[1]]
    planes = jnp.concatenate([plane.astype(F32) for plane in planes], axis=0)
    taps = shifts(planes, 256)
    taps = jnp.concatenate(taps + [jnp.zeros((40, 2048), F32)], axis=0)
    taps_one[...] = taps.astype(BF16)
    active, slope = activate(mm(weight_one[...], taps_one[...]))
    slope_one[...] = slope
    deep = jnp.concatenate(
        [active[0:32] + active[32:64], active[64:96] + active[96:128]], axis=0
    )
    pool = pool_matrix((256, 128), 256)
    for y in range(4):
        low = deep[:, y * 512 : y * 512 + 256]
        high = deep[:, y * 512 + 256 : y * 512 + 512]
        pooled = (mm2(low + high, pool) * 0.125).astype(BF16)
        rim_one[1, :, y * 128 : y * 128 + 128] = pooled[0:32]
        rim_one[2, :, y * 128 : y * 128 + 128] = pooled[32:64]

    edge = halo(1, rim_one.at[1], rim_one.at[2], rim_one.at[0], rim_one.at[3])
    for z in (1, 2):
        lay_taps(taps_two, z * 288, rim_one[z], 128)
    edge.wait()
    for z in (0, 3):
        lay_taps(taps_two, z * 288, rim_one[z], 128)
    kernel_two = weight_two[...].reshape(864, 64)
    pairs = [activate(tn(kernel_two, taps_two[z * 288 : z * 288 + 864, :])) for z in range(2)]
    slope_two = [pair[1] for pair in pairs]
    pool = pool_matrix((512, 128), 128)
    rim_two[1] = (mm2(pairs[0][0] + pairs[1][0], pool) * 0.125).astype(BF16)

    edge = halo(2, rim_two.at[1], rim_two.at[1], rim_two.at[0], rim_two.at[2])
    lay_taps(taps_three, 576, rim_two[1], 64)
    finish(cots)
    cot = jnp.concatenate([cot_all[i] for i in range(n)], axis=0).astype(BF16)
    wide = mm(cot, pool_matrix((32, 128), 64, True)) * 0.125
    edge.wait()
    for z in (0, 2):
        lay_taps(taps_three, z * 576, rim_two[z], 64)
    kernel_three = weight_three[...].reshape(1728, 128)
    active, slope = activate(tn(kernel_three, taps_three[0:1728, :]))
    grad = (wide * slope).astype(BF16)
    rim_three[1] = grad

    edge = halo(3, rim_three.at[1], rim_three.at[1], rim_three.at[0], rim_three.at[2])
    lay_taps(wide_three, 1152, grad, 64)
    for part in range(4):
        term = mnt(grad, taps_three[part * 512 : part * 512 + 512, :])
        for i in range(n):
            a_src[part, i] = term[i * share : i * share + share].astype(BF16)
    a_slot[d] = a_src[d]
    a_first = spread(1, "dp", lambda p: a_src.at[p], a_slot.at[d])
    paired = mm2(active, pool_matrix((128, 32), 64))
    for i in range(n):
        p_src[i] = paired[i * share : i * share + share]
    p_out[s] = p_src[s]
    feats = spread(2, "space", lambda p: p_src.at[p], p_out.at[s])
    edge.wait()
    for z in (0, 2):
        lay_taps(wide_three, z * 1152, rim_three[z], 64)
    flipped = jnp.concatenate([weight_three[26 - t] for t in range(27)], axis=1)
    back = mm(flipped, wide_three[...])
    wide = mm2(back, pool_matrix((128, 512), 128, True)) * 0.125
    grads = [(wide * slope_two[z]).astype(BF16) for z in range(2)]
    for z in range(2):
        rim_four[z + 1] = grads[z]

    edge = halo(4, rim_four.at[1], rim_four.at[2], rim_four.at[0], rim_four.at[3])
    total = mnt(grads[0], taps_two[0:896, :]) + mnt(grads[1], taps_two[288:1184, :])
    stack = jnp.concatenate([total[:, k * 128 : k * 128 + 128] for k in range(7)], axis=0)
    rows = b_src.shape[2]
    for i in range(nd * n):
        piece = stack[i * rows : i * rows + rows]
        if piece.shape[0] < rows:
            piece = jnp.zeros((rows, 128), F32)
        b_src[i // n, i % n] = piece
    b_slot[d] = b_src[d]
    b_first = spread(3, "dp", lambda p: b_src.at[p], b_slot.at[d])
    for z in (1, 2):
        lay_taps(wide_two, z * 576, rim_four[z], 128)
    finish(a_first)
    a_sum[...] = added(a_slot, nd)
    a_next[s] = a_sum[s]
    a_second = spread(4, "space", lambda p: a_sum.at[p], a_next.at[s])
    edge.wait()
    for z in (0, 3):
        lay_taps(wide_two, z * 576, rim_four[z], 128)
    backs = [mm(back_two[...], wide_two[z * 576 : z * 576 + 1728, :]) for z in range(2)]
    pool = pool_matrix((128, 256), 256, True)
    for y in range(4):
        wides = [mm2(back[:, y * 128 : y * 128 + 128], pool) * 0.125 for back in backs]
        wide = jnp.concatenate([wides[0], wides[0], wides[1], wides[1]], axis=0)
        for part in range(2):
            at = y * 512 + part * 256
            grad_one[:, at : at + 256] = (wide * slope_one[:, at : at + 256]).astype(BF16)
    total = mnt(grad_one[...], taps_one[...])
    result = total[0:32]
    for z in range(1, 4):
        result = result + pltpu.roll(total[32 * z : 32 * z + 32], 256 - 4 * z, 1)
    c_src[...] = jnp.concatenate([result[:, 0:128], result[:, 128:256]], axis=0)
    c_slot[d] = c_src[...]
    c_first = spread(5, "dp", lambda p: c_src, c_slot.at[d])

    finish(b_first)
    b_sum[...] = added(b_slot, nd)
    b_next[s] = b_sum[s]
    b_second = spread(6, "space", lambda p: b_sum.at[p], b_next.at[s])
    finish(c_first)
    total = added(c_slot, nd)
    rows = c_sum.shape[1]
    for i in range(n):
        piece = total[i * rows : i * rows + rows]
        if piece.shape[0] < rows:
            piece = jnp.zeros((rows, 128), F32)
        c_sum[i] = piece
    c_next[s] = c_sum[s]
    c_second = spread(7, "space", lambda p: c_sum.at[p], c_next.at[s])
    finish(a_second)
    a_out[d] = added(a_next, n)
    a_third = spread(8, "dp", lambda p: a_out.at[d], a_out.at[d])
    finish(b_second)
    b_mid[d] = added(b_next, n)
    b_third = spread(9, "dp", lambda p: b_mid.at[d], b_mid.at[d])
    finish(c_second)
    c_out[s] = added(c_next, n)
    c_third = spread(10, "space", lambda p: c_out.at[s], c_out.at[s])
    finish(b_third)
    b_out[s] = b_mid[...]
    b_last = spread(11, "space", lambda p: b_mid, b_out.at[s])
    for copies in (feats, a_third, c_third, b_last):
        finish(copies)


def banded(weight, planes):
    taps, in_width, out_width = weight.shape
    kernel = weight.reshape(3, 9, in_width, out_width).transpose(3, 1, 0, 2)
    rows = [
        jnp.pad(kernel, ((0, 0), (0, 0), (z, planes - 1 - z), (0, 0))) for z in range(planes)
    ]
    return jnp.stack(rows).reshape(planes * out_width, 9 * (planes + 2) * in_width)


def body(nd, n, volume, first_weight, second_weight, third_weight, feature_cotangent):
    share = feature_cotangent.shape[1]
    depth = feature_cotangent.shape[2]
    planes = volume[0].transpose(1, 0, 2, 3).reshape(4, 4, 2048)
    weight_one = jnp.pad(banded(first_weight, 4), ((0, 0), (0, 40)))
    cotangent = feature_cotangent[0].transpose(1, 0, 2).astype(F32)
    b_rows = pl.cdiv(448, nd * n)
    c_rows = pl.cdiv(64, n)
    most = max(nd, n)
    scratch = [
        ((2, 4, 2048), BF16), ((4, 32, 512), BF16), ((3, 64, 128), BF16), ((3, 128, 128), BF16),
        ((4, 64, 512), BF16), ((n, share, 32), F32),
        ((256, 2048), BF16), ((1184, 512), BF16), ((2048, 128), BF16), ((3456, 128), BF16),
        ((2304, 512), BF16), ((128, 2048), F32), ((128, 2048), BF16), ((32, 1728), BF16),
        ((n, share, 32), F32), ((nd, n, share, 512), BF16), ((nd, n, share, 512), BF16),
        ((n, share, 512), F32), ((n, share, 512), F32),
        ((nd, n, b_rows, 128), F32), ((nd, n, b_rows, 128), F32), ((n, b_rows, 128), F32),
        ((n, b_rows, 128), F32), ((nd, b_rows, 128), F32),
        ((64, 128), F32), ((nd, 64, 128), F32), ((n, c_rows, 128), F32), ((n, c_rows, 128), F32),
    ]
    third, rest, first, turned = pl.pallas_call(
        functools.partial(step_kernel, nd, n, share),
        out_shape=[
            jax.ShapeDtypeStruct((nd, share, 512), F32),
            jax.ShapeDtypeStruct((n, nd, b_rows, 128), F32),
            jax.ShapeDtypeStruct((n, c_rows, 128), F32),
            jax.ShapeDtypeStruct((n, share, 32), F32),
        ],
        in_specs=[VM] * 5,
        out_specs=[VM] * 4,
        scratch_shapes=[pltpu.VMEM(shape, kind) for shape, kind in scratch]
        + [pltpu.SemaphoreType.DMA((5, 2))] * 2
        + [pltpu.SemaphoreType.DMA((12, most))] * 2,
        compiler_params=pltpu.CompilerParams(
            collective_id=1, has_side_effects=True, vmem_limit_bytes=56 << 20
        ),
    )(planes, weight_one, second_weight, third_weight, cotangent)

    features = turned.reshape(depth, 2, share, 32).sum(axis=1) * 0.125
    features = features.transpose(1, 0, 2).astype(BF16)[None]
    third = third.transpose(1, 0, 2).reshape(share, 2048)[:, :1728]
    third_grad = third.reshape(share, 27, 64).transpose(1, 2, 0)
    rest = rest.transpose(1, 0, 2, 3).reshape(nd * n * b_rows, 128)[:448]
    second = rest.reshape(7, 64, 128).transpose(1, 0, 2).reshape(64, 896)[:, :864]
    second_grad = second.T.reshape(27, 32, 64)
    first = first.reshape(n * c_rows, 128)[:64]
    first = first.reshape(2, 32, 128).transpose(1, 0, 2).reshape(32, 256)
    first = first[:, :216].reshape(32, 9, 6, 4)[:, :, :3]
    first_grad = first.transpose(2, 1, 3, 0).reshape(27, 4, 32)
    return (features, first_grad, second_grad, third_grad)


def solution(mesh):
    return jax.shard_map(
        functools.partial(body, mesh.shape["dp"], mesh.shape["space"]),
        mesh=mesh,
        in_specs=(P("dp", None, "space", None, None), P(), P(), P(), P("dp", "space", None, None)),
        out_specs=(P("dp", "space", None, None), P(), P(), P(None, None, "space")),
        check_vma=False,
    )
```

time: 112 us -> 58.8 us (0.53)
  the two profiles are of different devices: /device:TPU:26 before, /device:TPU:0 now
where the time goes in v1:
time: 58.8 us; the launch traced here: 58.3 us
  Pallas kernels  48.6 us (83%)
  local copies, waits for them, and re-layouts  6.53 us (11%)
  other arithmetic  2.42 us (4%)
  between operations  0.78 us (1%)
    pallas_call x1, Pallas kernels, body(): pl.pallas_call(functools.partial(step_kernel, nd, n, share), out_shape=[j...  48.6 us
    unnamed x11, local copies, waits for them, and re-layouts  2.01 us
    reshape x2, local copies, waits for them, and re-layouts, body(): planes = volume[0].transpose(1, 0, 2, 3).reshape(4, 4, 2048)  1.55 us
    convert_element_type x1, other arithmetic, body(): cotangent = feature_cotangent[0].transpose(1, 0, 2).astype(F32)  1.34 us

profile of v1, /device:TPU:0, one launch (start us, length us, event | category | flops | bytes accessed | tf_op | source)
XLA Modules:
  0.0 58.3 jit_solution(17744102904351985961)
XLA Ops:
  0.6 1.3 %convert_bitcast_fusion.cotangent = f32[4,16,32]{2,1,0:T(8,128)} fusion(bf16[1,16,4,32]{3,2,1,0:T(4,128)(2,1)} %param.9), kind=kLoop, calls=%fused_computation.10 | loop fusion | flops 2048 | bytes 12288 | tf_op jit(solution)/shard_map/convert_element_type | solution.py:349
  2.0 0.9 %reshape.55 = bf16[4,4,2048]{2,0,1:T(4,128)(2,1)S(1)} reshape(bf16[4,4,8,256]{3,2,0,1:T(8,128)(2,1)} %bitcast.64) | data formatting | bytes 131072 | tf_op jit(solution)/shard_map/reshape | solution.py:347
  2.8 0.0 copy-start.3
  2.9 0.7 %copy.65.volume = bf16[4,4,2048]{2,1,0:T(4,128)(2,1)} copy(bf16[4,4,2048]{2,0,1:T(4,128)(2,1)S(1)} %reshape.55) | data formatting | bytes 131072 | tf_op jit(solution)/shard_map/reshape | solution.py:347
  3.5 0.1 copy-done.3
  3.6 0.1 pad_bitcast_fusion.3
  3.7 0.2 pad_maximum_fusion
  3.9 0.1 copy.53
  4.0 0.2 reshape.45
  4.1 0.1 copy.54
  4.3 0.6 %pad.24.weight_one = bf16[128,256]{1,0:T(8,128)(2,1)} pad(bf16[128,216]{1,0:T(8,128)(2,1)S(1)} %copy.54, bf16[]{:T(256)} %constant.1.clone.1), padding=0_0x0_40 | pad | bytes 120834 | tf_op jit(solution)/shard_map/jit(_pad)/pad | solution.py:348
  4.9 48.6 %shard_map.84 = (f32[4,16,512]{2,1,0:T(8,128)}, f32[8,4,14,128]{3,2,1,0:T(8,128)}, f32[8,8,128]{2,1,0:T(8,128)}, f32[8,16,32]{2,1,0:T(8,128)}) custom-call(bf16[4,4,2048]{2,1,0:T(4,128)(2,1)} %copy.65.volume, bf16[128,256]{1,0:T(8,128)(2,1)} %pad.24.weight_one, bf16[27,32,64]{2,1,0:T(8,128)(2,1)} %weight_two.1, bf16[27,64,128]{2,1,0:T(8,128)(2,1)} %weight_three.1, ...), custom_call_target="tpu_custom_call" | custom-call | tf_op jit(solution)/shard_map/pallas_call | solution.py:364
  53.5 0.9 %bitcast_reduce_fusion = f32[4,16,32]{2,1,0:T(8,128)S(1)} fusion(f32[8,16,32]{2,1,0:T(8,128)} %get-tuple-element.8), kind=kLoop, calls=%fused_computation.3 | loop fusion | flops 2048 | bytes 24576 | tf_op jit(solution)/shard_map/reduce_sum | solution.py:382
  54.3 0.0 copy-start.2
  54.4 0.6 %copy.63 = bf16[1,16,4,32]{3,2,1,0:T(4,128)(2,1)} copy(bf16[1,16,4,32]{3,1,2,0:T(8,128)(2,1)S(1)} %fusion) | data formatting | bytes 8192
  55.0 0.1 copy-done.2
  55.1 0.1 copy.57
  55.2 0.0 copy-start.1
  55.3 0.6 %copy.58 = f32[3,9,4,32]{3,2,1,0:T(4,128)} copy(f32[3,9,4,32]{3,2,0,1:T(4,128)S(1)} %slice_bitcast_fusion.1) | data formatting | bytes 27648 | tf_op jit(solution)/shard_map/transpose | solution.py:392
  55.9 0.3 copy-done.1
  56.2 0.1 reshape.53
  56.3 0.0 copy-start
  56.3 0.8 %copy.64 = f32[27,64,16]{1,2,0:T(8,128)} copy(f32[27,64,16]{1,0,2:T(8,128)S(1)} %bitcast.56) | data formatting | bytes 221184
  57.1 0.1 copy-done
  57.3 1.0 %copy.61 = f32[864,64]{1,0:T(8,128)} copy(f32[864,64]{0,1:T(8,128)S(1)} %slice_bitcast_fusion) | data formatting | bytes 442368 | tf_op jit(solution)/shard_map/transpose | solution.py:388
  (10 shorter events, 0.1 us)
Async XLA Ops:
  2.8 0.7 %copy-start.3 = (bf16[27,4,32]{2,1,0:T(4,128)(2,1)S(1)}, bf16[27,4,32]{2,1,0:T(4,128)(2,1)}, u32[]{:S(2)}) copy-start(bf16[27,4,32]{2,1,0:T(4,128)(2,1)} %param.6) | copy-start | bytes 20740
  54.3 0.8 %copy-start.2 = (f32[8,8,128]{2,1,0:T(8,128)S(1)}, f32[8,8,128]{2,1,0:T(8,128)}, u32[]{:S(2)}) copy-start(f32[8,8,128]{2,1,0:T(8,128)} %get-tuple-element.9) | copy-start | bytes 98308
  55.2 0.9 %copy-start.1 = (f32[4,16,512]{2,1,0:T(8,128)S(1)}, f32[4,16,512]{2,1,0:T(8,128)}, u32[]{:S(2)}) copy-start(f32[4,16,512]{2,1,0:T(8,128)} %get-tuple-element.11) | copy-start | bytes 393220
  56.3 1.0 %copy-start = (f32[8,4,14,128]{3,2,1,0:T(8,128)S(1)}, f32[8,4,14,128]{3,2,1,0:T(8,128)}, u32[]{:S(2)}) copy-start(f32[8,4,14,128]{3,2,1,0:T(8,128)} %get-tuple-element.10) | copy-start | bytes 688132

commit v2 on v1

--- a/solution.py
+++ b/solution.py
@@ -2,6 +2,7 @@
 
 import jax
 import jax.numpy as jnp
+import numpy as np
 from jax import lax
 from jax.experimental import pallas as pl
 from jax.experimental.pallas import tpu as pltpu
@@ -172,12 +173,12 @@
 
 
 def step_kernel(
-    nd, n, share, volume, weight_one, weight_two, weight_three, cotangent,
+    nd, n, share, volume, weight_one, select, weight_two, weight_three, cotangent_in,
     a_out, b_out, c_out, p_out,
     rim_zero, rim_one, rim_two, rim_three, rim_four, cot_all,
     taps_one, taps_two, taps_three, wide_three, wide_two, slope_one, grad_one, back_two,
-    p_src, a_src, a_slot, a_sum, a_next, b_src, b_slot, b_sum, b_next, b_mid,
-    c_src, c_slot, c_sum, c_next, halo_send, halo_recv, sends, recvs,
+    p_src, a_src, a_got, a_half, a_other, a_sum, a_next, b_src, b_got, b_half, b_other, b_sum, b_next,
+    c_src, c_slot, c_sum, c_next, cotangent, inner, outer, halo_send, halo_recv, sends, recvs,
 ):
     d = lax.axis_index("dp")
     s = lax.axis_index("space")
@@ -191,21 +192,43 @@
             axis, nd if axis == "dp" else n, sends.at[index], recvs.at[index], source, target
         )
 
-    edge = halo(0, volume.at[0], volume.at[3], rim_zero.at[0], rim_zero.at[1])
+    core = lax.rem(d, 2)
+    row = lax.div(d, 2)
+    beside = d + 1 - 2 * core
+    across = lax.rem(d + 2, 4)
+
+    def pass_to(index, slot, peer, source, target):
+        copy = pltpu.make_async_remote_copy(
+            src_ref=source, dst_ref=target, send_sem=sends.at[index, slot],
+            recv_sem=recvs.at[index, slot], device_id={"dp": peer}, device_id_type=MESH,
+        )
+        copy.start()
+        return copy
+
+    edge = halo(0, volume.at[:, 0], volume.at[:, 3], rim_zero.at[0], rim_zero.at[1])
+    spots = cotangent_in[...].astype(F32)
+    for z in range(spots.shape[1]):
+        cotangent[z] = spots[:, z, :]
     cot_all[s] = cotangent[lax.div(s, 2)]
     cots = spread(0, "space", lambda p: cotangent.at[lax.div(p, 2)], cot_all.at[s])
     for t in range(27):
         back_two[:, t * 64 : t * 64 + 64] = weight_two[26 - t]
     taps_two[1152:1184, :] = jnp.zeros((32, 512), BF16)
     taps_three[1728:2048, :] = jnp.zeros((320, 128), BF16)
+    inner[...] = volume[...].astype(F32).reshape(16, 8, 256)
+    band = jnp.concatenate(
+        [mnt(weight_one[...], select[z * 256 : z * 256 + 256, :]) for z in range(4)], axis=0
+    ).astype(BF16)
     edge.wait()
 
-    planes = [rim_zero[0]] + [volume[z] for z in range(4)] + [rim_zero[1]]
-    planes = jnp.concatenate([plane.astype(F32) for plane in planes], axis=0)
+    outer[...] = rim_zero[...].astype(F32).reshape(8, 8, 256)
+    planes = jnp.concatenate(
+        [jnp.concatenate([inner[:, y, :], outer[:, y, :]], axis=0) for y in range(8)], axis=1
+    )
     taps = shifts(planes, 256)
     taps = jnp.concatenate(taps + [jnp.zeros((40, 2048), F32)], axis=0)
     taps_one[...] = taps.astype(BF16)
-    active, slope = activate(mm(weight_one[...], taps_one[...]))
+    active, slope = activate(mm(band, taps_one[...]))
     slope_one[...] = slope
     deep = jnp.concatenate(
         [active[0:32] + active[32:64], active[64:96] + active[96:128]], axis=0
@@ -249,14 +272,19 @@
         term = mnt(grad, taps_three[part * 512 : part * 512 + 512, :])
         for i in range(n):
             a_src[part, i] = term[i * share : i * share + share].astype(BF16)
-    a_slot[d] = a_src[d]
-    a_first = spread(1, "dp", lambda p: a_src.at[p], a_slot.at[d])
+    a_first = [
+        pass_to(1, i, beside, a_src.at[2 * i + 1 - core], a_got.at[i]) for i in range(2)
+    ]
     paired = mm2(active, pool_matrix((128, 32), 64))
     for i in range(n):
         p_src[i] = paired[i * share : i * share + share]
     p_out[s] = p_src[s]
     feats = spread(2, "space", lambda p: p_src.at[p], p_out.at[s])
     edge.wait()
+    finish(a_first)
+    for i in range(2):
+        a_half[i] = (a_src[2 * i + core].astype(F32) + a_got[i].astype(F32)).astype(BF16)
+    a_first = [pass_to(3, 0, across, a_half.at[1 - row], a_other)]
     for z in (0, 2):
         lay_taps(wide_three, z * 1152, rim_three[z], 64)
     flipped = jnp.concatenate([weight_three[26 - t] for t in range(27)], axis=1)
@@ -269,21 +297,18 @@
     edge = halo(4, rim_four.at[1], rim_four.at[2], rim_four.at[0], rim_four.at[3])
     total = mnt(grads[0], taps_two[0:896, :]) + mnt(grads[1], taps_two[288:1184, :])
     stack = jnp.concatenate([total[:, k * 128 : k * 128 + 128] for k in range(7)], axis=0)
-    rows = b_src.shape[2]
-    for i in range(nd * n):
-        piece = stack[i * rows : i * rows + rows]
-        if piece.shape[0] < rows:
-            piece = jnp.zeros((rows, 128), F32)
-        b_src[i // n, i % n] = piece
-    b_slot[d] = b_src[d]
-    b_first = spread(3, "dp", lambda p: b_src.at[p], b_slot.at[d])
+    b_src[...] = stack.astype(BF16)
+    b_first = [pass_to(5, 0, beside, b_src, b_got)]
     for z in (1, 2):
         lay_taps(wide_two, z * 576, rim_four[z], 128)
     finish(a_first)
-    a_sum[...] = added(a_slot, nd)
+    a_sum[...] = (a_half[row].astype(F32) + a_other[...].astype(F32)).astype(BF16)
     a_next[s] = a_sum[s]
     a_second = spread(4, "space", lambda p: a_sum.at[p], a_next.at[s])
     edge.wait()
+    finish(b_first)
+    b_half[...] = (b_src[...].astype(F32) + b_got[...].astype(F32)).astype(BF16)
+    b_first = [pass_to(6, 0, across, b_half, b_other)]
     for z in (0, 3):
         lay_taps(wide_two, z * 576, rim_four[z], 128)
     backs = [mm(back_two[...], wide_two[z * 576 : z * 576 + 1728, :]) for z in range(2)]
@@ -295,81 +320,81 @@
             at = y * 512 + part * 256
             grad_one[:, at : at + 256] = (wide * slope_one[:, at : at + 256]).astype(BF16)
     total = mnt(grad_one[...], taps_one[...])
-    result = total[0:32]
-    for z in range(1, 4):
-        result = result + pltpu.roll(total[32 * z : 32 * z + 32], 256 - 4 * z, 1)
-    c_src[...] = jnp.concatenate([result[:, 0:128], result[:, 128:256]], axis=0)
+    c_src[...] = sum(
+        mm2(total[32 * z : 32 * z + 32], select[z * 256 : z * 256 + 256, :]) for z in range(4)
+    )
     c_slot[d] = c_src[...]
-    c_first = spread(5, "dp", lambda p: c_src, c_slot.at[d])
+    c_first = spread(7, "dp", lambda p: c_src, c_slot.at[d])
 
     finish(b_first)
-    b_sum[...] = added(b_slot, nd)
-    b_next[s] = b_sum[s]
-    b_second = spread(6, "space", lambda p: b_sum.at[p], b_next.at[s])
-    finish(c_first)
-    total = added(c_slot, nd)
-    rows = c_sum.shape[1]
+    total = b_half[...].astype(F32) + b_other[...].astype(F32)
+    rows = b_sum.shape[1]
     for i in range(n):
         piece = total[i * rows : i * rows + rows]
         if piece.shape[0] < rows:
             piece = jnp.zeros((rows, 128), F32)
-        c_sum[i] = piece
-    c_next[s] = c_sum[s]
-    c_second = spread(7, "space", lambda p: c_sum.at[p], c_next.at[s])
+        b_sum[i] = piece.astype(BF16)
+    b_next[s] = b_sum[s]
+    b_second = spread(8, "space", lambda p: b_sum.at[p], b_next.at[s])
+    finish(c_first)
+    c_sum[...] = added(c_slot, nd)
+    c_next[s] = c_sum[...]
+    c_second = spread(9, "space", lambda p: c_sum, c_next.at[s])
     finish(a_second)
     a_out[d] = added(a_next, n)
-    a_third = spread(8, "dp", lambda p: a_out.at[d], a_out.at[d])
+    a_third = spread(10, "dp", lambda p: a_out.at[d], a_out.at[d])
     finish(b_second)
-    b_mid[d] = added(b_next, n)
-    b_third = spread(9, "dp", lambda p: b_mid.at[d], b_mid.at[d])
+    b_out[s] = added(b_next, n).astype(BF16)
+    b_third = spread(11, "space", lambda p: b_out.at[s], b_out.at[s])
     finish(c_second)
-    c_out[s] = added(c_next, n)
-    c_third = spread(10, "space", lambda p: c_out.at[s], c_out.at[s])
-    finish(b_third)
-    b_out[s] = b_mid[...]
-    b_last = spread(11, "space", lambda p: b_mid, b_out.at[s])
-    for copies in (feats, a_third, c_third, b_last):
+    c_out[...] = added(c_next, n)
+    for copies in (feats, a_third, b_third):
         finish(copies)
 
 
-def banded(weight, planes):
-    taps, in_width, out_width = weight.shape
-    kernel = weight.reshape(3, 9, in_width, out_width).transpose(3, 1, 0, 2)
-    rows = [
-        jnp.pad(kernel, ((0, 0), (0, 0), (z, planes - 1 - z), (0, 0))) for z in range(planes)
-    ]
-    return jnp.stack(rows).reshape(planes * out_width, 9 * (planes + 2) * in_width)
+def select_taps():
+    table = np.zeros((4, 9, 24, 27, 4), np.float32)
+    for z in range(4):
+        for spot in range(24):
+            if spot < 16:
+                channel, plane = spot // 4, spot % 4 + 1
+            else:
+                channel, plane = spot % 4, 0 if spot < 20 else 5
+            if 0 <= plane - z < 3:
+                for k in range(9):
+                    table[z, k, spot, (plane - z) * 9 + k, channel] = 1.0
+    table = np.pad(table.reshape(4, 216, 108), ((0, 0), (0, 40), (0, 20)))
+    return jnp.asarray(table.reshape(1024, 128), BF16)
 
 
 def body(nd, n, volume, first_weight, second_weight, third_weight, feature_cotangent):
     share = feature_cotangent.shape[1]
     depth = feature_cotangent.shape[2]
-    planes = volume[0].transpose(1, 0, 2, 3).reshape(4, 4, 2048)
-    weight_one = jnp.pad(banded(first_weight, 4), ((0, 0), (0, 40)))
-    cotangent = feature_cotangent[0].transpose(1, 0, 2).astype(F32)
-    b_rows = pl.cdiv(448, nd * n)
-    c_rows = pl.cdiv(64, n)
+    weight_one = jnp.pad(first_weight.reshape(108, 32).T, ((0, 0), (0, 20)))
+    b_rows = pl.cdiv(448, n)
     most = max(nd, n)
     scratch = [
-        ((2, 4, 2048), BF16), ((4, 32, 512), BF16), ((3, 64, 128), BF16), ((3, 128, 128), BF16),
+        ((2, 4, 8, 256), BF16), ((4, 32, 512), BF16), ((3, 64, 128), BF16), ((3, 128, 128), BF16),
         ((4, 64, 512), BF16), ((n, share, 32), F32),
         ((256, 2048), BF16), ((1184, 512), BF16), ((2048, 128), BF16), ((3456, 128), BF16),
         ((2304, 512), BF16), ((128, 2048), F32), ((128, 2048), BF16), ((32, 1728), BF16),
-        ((n, share, 32), F32), ((nd, n, share, 512), BF16), ((nd, n, share, 512), BF16),
-        ((n, share, 512), F32), ((n, share, 512), F32),
-        ((nd, n, b_rows, 128), F32), ((nd, n, b_rows, 128), F32), ((n, b_rows, 128), F32),
-        ((n, b_rows, 128), F32), ((nd, b_rows, 128), F32),
-        ((64, 128), F32), ((nd, 64, 128), F32), ((n, c_rows, 128), F32), ((n, c_rows, 128), F32),
+        ((n, share, 32), F32), ((nd, n, share, 512), BF16), ((2, n, share, 512), BF16),
+        ((2, n, share, 512), BF16), ((n, share, 512), BF16), ((n, share, 512), BF16),
+        ((n, share, 512), BF16),
+        ((448, 128), BF16), ((448, 128), BF16), ((448, 128), BF16), ((448, 128), BF16),
+        ((n, b_rows, 128), BF16), ((n, b_rows, 128), BF16),
+        ((32, 128), F32), ((nd, 32, 128), F32), ((32, 128), F32), ((n, 32, 128), F32),
+        ((depth, share, 32), F32), ((16, 8, 256), F32), ((8, 8, 256), F32),
     ]
     third, rest, first, turned = pl.pallas_call(
         functools.partial(step_kernel, nd, n, share),
         out_shape=[
             jax.ShapeDtypeStruct((nd, share, 512), F32),
-            jax.ShapeDtypeStruct((n, nd, b_rows, 128), F32),
-            jax.ShapeDtypeStruct((n, c_rows, 128), F32),
+            jax.ShapeDtypeStruct((n, b_rows, 128), BF16),
+            jax.ShapeDtypeStruct((32, 128), F32),
             jax.ShapeDtypeStruct((n, share, 32), F32),
         ],
-        in_specs=[VM] * 5,
+        in_specs=[VM] * 6,
         out_specs=[VM] * 4,
         scratch_shapes=[pltpu.VMEM(shape, kind) for shape, kind in scratch]
         + [pltpu.SemaphoreType.DMA((5, 2))] * 2
@@ -377,19 +402,16 @@
         compiler_params=pltpu.CompilerParams(
             collective_id=1, has_side_effects=True, vmem_limit_bytes=56 << 20
         ),
-    )(planes, weight_one, second_weight, third_weight, cotangent)
+    )(volume[0], weight_one, select_taps(), second_weight, third_weight, feature_cotangent[0])
 
     features = turned.reshape(depth, 2, share, 32).sum(axis=1) * 0.125
     features = features.transpose(1, 0, 2).astype(BF16)[None]
     third = third.transpose(1, 0, 2).reshape(share, 2048)[:, :1728]
     third_grad = third.reshape(share, 27, 64).transpose(1, 2, 0)
-    rest = rest.transpose(1, 0, 2, 3).reshape(nd * n * b_rows, 128)[:448]
+    rest = rest.reshape(n * b_rows, 128)[:448]
     second = rest.reshape(7, 64, 128).transpose(1, 0, 2).reshape(64, 896)[:, :864]
-    second_grad = second.T.reshape(27, 32, 64)
-    first = first.reshape(n * c_rows, 128)[:64]
-    first = first.reshape(2, 32, 128).transpose(1, 0, 2).reshape(32, 256)
-    first = first[:, :216].reshape(32, 9, 6, 4)[:, :, :3]
-    first_grad = first.transpose(2, 1, 3, 0).reshape(27, 4, 32)
+    second_grad = second.T.reshape(27, 32, 64).astype(F32)
+    first_grad = first[:, :108].T.reshape(27, 4, 32)
     return (features, first_grad, second_grad, third_grad)
 
 

time: 58.8 us -> 54.3 us (0.923)
  Pallas kernels: 48.6 us -> 46.5 us
  other arithmetic: 2.42 us -> 0.88 us
  local copies, waits for them, and re-layouts: 6.53 us -> 5.94 us
    pallas_call x1, Pallas kernels: 48.6 us -> 46.5 us  [body(): pl.pallas_call(functools.partial(step_kernel, nd, n, share), out_shape=[j...]
    transpose x5 -> x2, local copies, waits for them, and re-layouts: 1.64 us -> 0.11 us  [body(): first_grad = first[:, :108].T.reshape(27, 4, 32)]
    convert_element_type x1, other arithmetic: 1.34 us -> 0.02 us  [body(): second_grad = second.T.reshape(27, 32, 64).astype(F32)]
    convert_element_type x0 -> x1, local copies, waits for them, and re-layouts: none -> 0.96 us  [body(): second_grad = second.T.reshape(27, 32, 64).astype(F32)]
    unnamed x11 -> x9, local copies, waits for them, and re-layouts: 2.01 us -> 2.56 us
    reshape x5 -> x3, local copies, waits for them, and re-layouts: 1.83 us -> 1.49 us  [the longest x2 0.85 us: body(): weight_one = jnp.pad(first_weight.reshape(108, 32).T, ((0, 0), (0, 20)))]
where the time goes in v2:
time: 54.3 us; the launch traced here: 54 us
  Pallas kernels  46.5 us (86%)
  local copies, waits for them, and re-layouts  5.94 us (11%)
  other arithmetic  0.88 us (2%)
  between operations  0.7 us (1%)
    pallas_call x1, Pallas kernels, body(): pl.pallas_call(functools.partial(step_kernel, nd, n, share), out_shape=[j...  46.5 us
    unnamed x9, local copies, waits for them, and re-layouts  2.56 us

profile of v2, /device:TPU:0, one launch (start us, length us, event | category | flops | bytes accessed | tf_op | source)
XLA Modules:
  0.0 54.0 jit_solution(15165243597867156644)
XLA Ops:
  0.6 0.8 %reshape.29 = bf16[108,32]{1,0:T(8,128)(2,1)S(1)} reshape(bf16[27,4,32]{2,1,0:T(4,128)(2,1)} %param.7) | data formatting | bytes 13824 | tf_op jit(solution)/shard_map/reshape | solution.py:373
  1.4 0.1 copy.24
  1.5 0.6 %pad.4.weight_one = bf16[32,128]{1,0:T(8,128)(2,1)} pad(bf16[32,108]{1,0:T(8,128)(2,1)S(1)} %bitcast.32, bf16[]{:T(256)} %constant.2.clone.1), padding=0_0x0_20 | pad | bytes 15106 | tf_op jit(solution)/shard_map/jit(_pad)/pad | solution.py:373
  2.1 46.5 %shard_map.93 = (f32[4,16,512]{2,1,0:T(8,128)}, bf16[8,56,128]{2,1,0:T(8,128)(2,1)}, f32[32,128]{1,0:T(8,128)}, f32[8,16,32]{2,1,0:T(8,128)}) custom-call(bf16[4,4,8,256]{3,2,1,0:T(8,128)(2,1)} %bitcast.31, bf16[32,128]{1,0:T(8,128)(2,1)} %pad.4.weight_one, bf16[1024,128]{1,0:T(8,128)(2,1)} %constant.9.clone.select, bf16[27,32,64]{2,1,0:T(8,128)(2,1)} %weight_two.1, ...), custom_call_target="tpu_custom_call" | custom-call | tf_op jit(solution)/shard_map/pallas_call | solution.py:389
  48.6 0.9 %bitcast_reduce_fusion = f32[4,16,32]{2,1,0:T(8,128)S(1)} fusion(f32[8,16,32]{2,1,0:T(8,128)} %get-tuple-element.8), kind=kLoop, calls=%fused_computation.2 | loop fusion | flops 2048 | bytes 24576 | tf_op jit(solution)/shard_map/reduce_sum | solution.py:407
  49.5 0.0 copy-start.2
  49.5 0.6 %copy.29 = bf16[1,16,4,32]{3,2,1,0:T(4,128)(2,1)} copy(bf16[1,16,4,32]{3,1,2,0:T(8,128)(2,1)S(1)} %fusion) | data formatting | bytes 8192
  50.1 0.1 copy-done.2
  50.2 0.0 copy-start.1
  50.2 0.1 copy.25
  50.3 0.6 %reshape.31 = f32[27,4,32]{2,1,0:T(4,128)} reshape(f32[108,32]{1,0:T(8,128)S(1)} %copy.25) | data formatting | bytes 27648 | tf_op jit(solution)/shard_map/reshape | solution.py:414
  50.9 0.1 copy-done.1
  51.1 0.1 copy.26
  51.2 0.0 copy-start
  51.2 0.9 %copy-done = f32[4,16,512]{2,1,0:T(8,128)S(1)} copy-done((f32[4,16,512]{2,1,0:T(8,128)S(1)}, f32[4,16,512]{2,1,0:T(8,128)}, u32[]{:S(2)}) %copy-start) | copy-done | bytes 131096
  52.1 0.1 reshape.34
  52.2 0.8 %copy.30 = f32[27,64,16]{1,2,0:T(8,128)} copy(f32[27,64,16]{1,0,2:T(8,128)S(1)} %bitcast.24) | data formatting | bytes 221184
  53.0 1.0 %copy.27 = f32[864,64]{1,0:T(8,128)} copy(f32[864,64]{0,1:T(8,128)S(1)} %convert_bitcast_fusion) | data formatting | bytes 442368 | tf_op jit(solution)/shard_map/convert_element_type | solution.py:413
  (6 shorter events, 0.1 us)
Async XLA Ops:
  49.5 0.7 %copy-start.2 = (f32[32,128]{1,0:T(8,128)S(1)}, f32[32,128]{1,0:T(8,128)}, u32[]{:S(2)}) copy-start(f32[32,128]{1,0:T(8,128)} %get-tuple-element.9) | copy-start | bytes 49156
  50.2 0.9 %copy-start.1 = (bf16[8,56,128]{2,1,0:T(8,128)(2,1)S(1)}, bf16[8,56,128]{2,1,0:T(8,128)(2,1)}, u32[]{:S(2)}) copy-start(bf16[8,56,128]{2,1,0:T(8,128)(2,1)} %get-tuple-element.10) | copy-start | bytes 344068
  51.2 0.9 %copy-start = (f32[4,16,512]{2,1,0:T(8,128)S(1)}, f32[4,16,512]{2,1,0:T(8,128)}, u32[]{:S(2)}) copy-start(f32[4,16,512]{2,1,0:T(8,128)} %get-tuple-element.11) | copy-start | bytes 393220

commit v3 on v2

--- a/solution.py
+++ b/solution.py
@@ -173,12 +173,12 @@
 
 
 def step_kernel(
-    nd, n, share, volume, weight_one, select, weight_two, weight_three, cotangent_in,
+    nd, n, share, volume, weight_one, select, weight_two, weight_three, cotangent,
     a_out, b_out, c_out, p_out,
     rim_zero, rim_one, rim_two, rim_three, rim_four, cot_all,
     taps_one, taps_two, taps_three, wide_three, wide_two, slope_one, grad_one, back_two,
     p_src, a_src, a_got, a_half, a_other, a_sum, a_next, b_src, b_got, b_half, b_other, b_sum, b_next,
-    c_src, c_slot, c_sum, c_next, cotangent, inner, outer, halo_send, halo_recv, sends, recvs,
+    c_src, c_slot, c_sum, c_next, halo_send, halo_recv, sends, recvs,
 ):
     d = lax.axis_index("dp")
     s = lax.axis_index("space")
@@ -205,26 +205,20 @@
         copy.start()
         return copy
 
-    edge = halo(0, volume.at[:, 0], volume.at[:, 3], rim_zero.at[0], rim_zero.at[1])
-    spots = cotangent_in[...].astype(F32)
-    for z in range(spots.shape[1]):
-        cotangent[z] = spots[:, z, :]
+    edge = halo(0, volume.at[0], volume.at[3], rim_zero.at[0], rim_zero.at[1])
     cot_all[s] = cotangent[lax.div(s, 2)]
     cots = spread(0, "space", lambda p: cotangent.at[lax.div(p, 2)], cot_all.at[s])
     for t in range(27):
         back_two[:, t * 64 : t * 64 + 64] = weight_two[26 - t]
     taps_two[1152:1184, :] = jnp.zeros((32, 512), BF16)
     taps_three[1728:2048, :] = jnp.zeros((320, 128), BF16)
-    inner[...] = volume[...].astype(F32).reshape(16, 8, 256)
     band = jnp.concatenate(
         [mnt(weight_one[...], select[z * 256 : z * 256 + 256, :]) for z in range(4)], axis=0
     ).astype(BF16)
     edge.wait()
 
-    outer[...] = rim_zero[...].astype(F32).reshape(8, 8, 256)
-    planes = jnp.concatenate(
-        [jnp.concatenate([inner[:, y, :], outer[:, y, :]], axis=0) for y in range(8)], axis=1
-    )
+    planes = [rim_zero[0]] + [volume[z] for z in range(4)] + [rim_zero[1]]
+    planes = jnp.concatenate([plane.astype(F32) for plane in planes], axis=0)
     taps = shifts(planes, 256)
     taps = jnp.concatenate(taps + [jnp.zeros((40, 2048), F32)], axis=0)
     taps_one[...] = taps.astype(BF16)
@@ -356,10 +350,7 @@
     table = np.zeros((4, 9, 24, 27, 4), np.float32)
     for z in range(4):
         for spot in range(24):
-            if spot < 16:
-                channel, plane = spot // 4, spot % 4 + 1
-            else:
-                channel, plane = spot % 4, 0 if spot < 20 else 5
+            channel, plane = spot % 4, spot // 4
             if 0 <= plane - z < 3:
                 for k in range(9):
                     table[z, k, spot, (plane - z) * 9 + k, channel] = 1.0
@@ -371,10 +362,12 @@
     share = feature_cotangent.shape[1]
     depth = feature_cotangent.shape[2]
     weight_one = jnp.pad(first_weight.reshape(108, 32).T, ((0, 0), (0, 20)))
+    planes = volume[0].transpose(1, 0, 2, 3).reshape(4, 4, 2048)
+    cotangent = feature_cotangent[0].transpose(1, 0, 2).astype(F32)
     b_rows = pl.cdiv(448, n)
     most = max(nd, n)
     scratch = [
-        ((2, 4, 8, 256), BF16), ((4, 32, 512), BF16), ((3, 64, 128), BF16), ((3, 128, 128), BF16),
+        ((2, 4, 2048), BF16), ((4, 32, 512), BF16), ((3, 64, 128), BF16), ((3, 128, 128), BF16),
         ((4, 64, 512), BF16), ((n, share, 32), F32),
         ((256, 2048), BF16), ((1184, 512), BF16), ((2048, 128), BF16), ((3456, 128), BF16),
         ((2304, 512), BF16), ((128, 2048), F32), ((128, 2048), BF16), ((32, 1728), BF16),
@@ -384,7 +377,6 @@
         ((448, 128), BF16), ((448, 128), BF16), ((448, 128), BF16), ((448, 128), BF16),
         ((n, b_rows, 128), BF16), ((n, b_rows, 128), BF16),
         ((32, 128), F32), ((nd, 32, 128), F32), ((32, 128), F32), ((n, 32, 128), F32),
-        ((depth, share, 32), F32), ((16, 8, 256), F32), ((8, 8, 256), F32),
     ]
     third, rest, first, turned = pl.pallas_call(
         functools.partial(step_kernel, nd, n, share),
@@ -402,7 +394,7 @@
         compiler_params=pltpu.CompilerParams(
             collective_id=1, has_side_effects=True, vmem_limit_bytes=56 << 20
         ),
-    )(volume[0], weight_one, select_taps(), second_weight, third_weight, feature_cotangent[0])
+    )(planes, weight_one, select_taps(), second_weight, third_weight, cotangent)
 
     features = turned.reshape(depth, 2, share, 32).sum(axis=1) * 0.125
     features = features.transpose(1, 0, 2).astype(BF16)[None]

time: 54.3 us -> 55.7 us (1.026)
  local copies, waits for them, and re-layouts: 5.94 us -> 6.67 us
  other arithmetic: 0.88 us -> 1.5 us
    reshape x0 -> x2, local copies, waits for them, and re-layouts: none -> 0.72 us  [body(): planes = volume[0].transpose(1, 0, 2, 3).reshape(4, 4, 2048)]
    convert_element_type x0 -> x1, other arithmetic: none -> 0.62 us  [body(): cotangent = feature_cotangent[0].transpose(1, 0, 2).astype(F32)]
    unnamed x9 -> x13, local copies, waits for them, and re-layouts: 2.56 us -> 2.57 us
where the time goes in v3:
time: 55.7 us; the launch traced here: 55.3 us
  Pallas kernels  46.4 us (83%)
  local copies, waits for them, and re-layouts  6.67 us (12%)
  other arithmetic  1.5 us (3%)
  between operations  0.73 us (1%)
    pallas_call x1, Pallas kernels, body(): pl.pallas_call(functools.partial(step_kernel, nd, n, share), out_shape=[j...  46.4 us
    unnamed x13, local copies, waits for them, and re-layouts  2.57 us

profile of v3, /device:TPU:0, one launch (start us, length us, event | category | flops | bytes accessed | tf_op | source)
XLA Modules:
  0.0 55.3 jit_solution(2242337596151523550)
XLA Ops:
  0.6 0.0 copy-start.3
  0.6 0.8 %reshape.35 = bf16[108,32]{1,0:T(8,128)(2,1)S(1)} reshape(bf16[27,4,32]{2,1,0:T(4,128)(2,1)} %param.7) | data formatting | bytes 13824 | tf_op jit(solution)/shard_map/reshape | solution.py:364
  1.4 0.0 copy-start.2
  1.4 0.1 copy.31
  1.5 0.6 %pad.4.weight_one = bf16[32,128]{1,0:T(8,128)(2,1)} pad(bf16[32,108]{1,0:T(8,128)(2,1)S(1)} %bitcast.42, bf16[]{:T(256)} %constant.2.clone.1), padding=0_0x0_20 | pad | bytes 15106 | tf_op jit(solution)/shard_map/jit(_pad)/pad | solution.py:364
  2.1 0.0 copy-done.3
  2.1 0.6 %convert_bitcast_fusion.1.cotangent = f32[4,16,32]{2,1,0:T(8,128)} fusion(bf16[1,16,4,32]{3,2,1,0:T(4,128)(2,1)S(1)} %copy-done.3), kind=kLoop, calls=%fused_computation.3 | loop fusion | flops 2048 | bytes 12288 | tf_op jit(solution)/shard_map/convert_element_type | solution.py:366
  2.8 0.0 copy-done.2
  2.8 0.7 %copy.39.volume = bf16[4,4,2048]{2,1,0:T(4,128)(2,1)} copy(bf16[4,4,2048]{2,0,1:T(4,128)(2,1)S(1)} %reshape.43) | data formatting | bytes 131072 | tf_op jit(solution)/shard_map/reshape | solution.py:365
  3.5 46.4 %shard_map.93 = (f32[4,16,512]{2,1,0:T(8,128)}, bf16[8,56,128]{2,1,0:T(8,128)(2,1)}, f32[32,128]{1,0:T(8,128)}, f32[8,16,32]{2,1,0:T(8,128)}) custom-call(bf16[4,4,2048]{2,1,0:T(4,128)(2,1)} %copy.39.volume, bf16[32,128]{1,0:T(8,128)(2,1)} %pad.4.weight_one, bf16[1024,128]{1,0:T(8,128)(2,1)} %constant.9.clone.select, bf16[27,32,64]{2,1,0:T(8,128)(2,1)} %weight_two.1, ...), custom_call_target="tpu_custom_call" | custom-call | tf_op jit(solution)/shard_map/pallas_call | solution.py:381
  49.9 0.9 %bitcast_reduce_fusion = f32[4,16,32]{2,1,0:T(8,128)S(1)} fusion(f32[8,16,32]{2,1,0:T(8,128)} %get-tuple-element.8), kind=kLoop, calls=%fused_computation.2 | loop fusion | flops 2048 | bytes 24576 | tf_op jit(solution)/shard_map/reduce_sum | solution.py:399
  50.8 0.0 copy-start.4
  50.8 0.6 %copy.37 = bf16[1,16,4,32]{3,2,1,0:T(4,128)(2,1)} copy(bf16[1,16,4,32]{3,1,2,0:T(8,128)(2,1)S(1)} %fusion) | data formatting | bytes 8192
  51.4 0.1 copy-done.4
  51.5 0.0 copy-start.1
  51.5 0.1 copy.33
  51.6 0.6 %reshape.37 = f32[27,4,32]{2,1,0:T(4,128)} reshape(f32[108,32]{1,0:T(8,128)S(1)} %copy.33) | data formatting | bytes 27648 | tf_op jit(solution)/shard_map/reshape | solution.py:406
  52.3 0.1 copy-done.1
  52.4 0.1 copy.34
  52.5 0.0 copy-start
  52.6 0.9 %copy-done = f32[4,16,512]{2,1,0:T(8,128)S(1)} copy-done((f32[4,16,512]{2,1,0:T(8,128)S(1)}, f32[4,16,512]{2,1,0:T(8,128)}, u32[]{:S(2)}) %copy-start) | copy-done | bytes 131096
  53.5 0.1 reshape.40
  53.6 0.8 %copy.38 = f32[27,64,16]{1,2,0:T(8,128)} copy(f32[27,64,16]{1,0,2:T(8,128)S(1)} %bitcast.34) | data formatting | bytes 221184
  54.4 1.0 %copy.35 = f32[864,64]{1,0:T(8,128)} copy(f32[864,64]{0,1:T(8,128)S(1)} %convert_bitcast_fusion) | data formatting | bytes 442368 | tf_op jit(solution)/shard_map/convert_element_type | solution.py:405
  (7 shorter events, 0.1 us)
Async XLA Ops:
  0.6 1.5 %copy-start.3 = (bf16[1,16,4,32]{3,2,1,0:T(4,128)(2,1)S(1)}, bf16[1,16,4,32]{3,2,1,0:T(4,128)(2,1)}, u32[]{:S(2)}) copy-start(bf16[1,16,4,32]{3,2,1,0:T(4,128)(2,1)} %param.10) | copy-start | bytes 12292
  1.4 1.3 %copy-start.2 = (bf16[1,4,4,8,256]{4,3,2,1,0:T(8,128)(2,1)S(1)}, bf16[1,4,4,8,256]{4,3,2,1,0:T(8,128)(2,1)}, u32[]{:S(2)}) copy-start(bf16[1,4,4,8,256]{4,3,2,1,0:T(8,128)(2,1)} %param.6) | copy-start | bytes 196612
  50.8 0.7 %copy-start.4 = (f32[32,128]{1,0:T(8,128)S(1)}, f32[32,128]{1,0:T(8,128)}, u32[]{:S(2)}) copy-start(f32[32,128]{1,0:T(8,128)} %get-tuple-element.9) | copy-start | bytes 49156
  51.5 0.9 %copy-start.1 = (bf16[8,56,128]{2,1,0:T(8,128)(2,1)S(1)}, bf16[8,56,128]{2,1,0:T(8,128)(2,1)}, u32[]{:S(2)}) copy-start(bf16[8,56,128]{2,1,0:T(8,128)(2,1)} %get-tuple-element.10) | copy-start | bytes 344068
  52.5 0.9 %copy-start = (f32[4,16,512]{2,1,0:T(8,128)S(1)}, f32[4,16,512]{2,1,0:T(8,128)}, u32[]{:S(2)}) copy-start(f32[4,16,512]{2,1,0:T(8,128)} %get-tuple-element.11) | copy-start | bytes 393220
